TPU v7x, 128 devices: a whole 4x4x4 slice. The times are simulated.
128 devices in a mesh: token: 8 (over y, core), tensor: 16 (over z, x).
Axes of the slice: x: 4, y: 4, z: 4, core: 2. Of those that a mesh axis runs over, the one named last changes fastest.
Arguments:
- tokens: bfloat16 [8192, 4096], P(('token', 'tensor')), may hold values from -6 to 6
- doc_lengths: int32 [4], replicated, may hold values from 1 to 4096, 8192 in all
- attn_gain: float32 [4096], replicated, may hold values from 0.1 to 1.9
- mlp_gain: float32 [4096], replicated, may hold values from 0.1 to 1.9
- w_query: bfloat16 [4096, 4096], P(None, 'tensor'), may hold values from -0.067528728 to 0.067528728
- w_keyval: bfloat16 [4096, 2048], P(None, 'tensor'), may hold values from -0.067528728 to 0.067528728
- w_out: bfloat16 [4096, 4096], P('tensor'), may hold values from -0.09375 to 0.09375
- w_gate: bfloat16 [4096, 7168], P(None, 'tensor'), may hold values from -0.09375 to 0.09375
- w_up: bfloat16 [4096, 7168], P(None, 'tensor'), may hold values from -0.09375 to 0.09375
- w_down: bfloat16 [7168, 4096], P('tensor'), may hold values from -0.0625 to 0.0625
Outputs:
- layer_out: bfloat16 [8192, 4096], P(('token', 'tensor'))
Inputs may be any that keep to these rules, and one draw needn't show every extreme that they name: `doc_lengths`: the lengths sum to 8192; exactly one document has length 4096, the largest allowed.
All inputs are finite; a program needn't handle non-finite values.
Results may differ from a plain program's by a relative error of at most 0.017.
Values may be sent and summed in bfloat16 or wider, within the bound.
A program may use at most 128 MiB of HBM per device.

v0:
```python
import math

import jax
import jax.numpy as jnp
from jax import lax
from jax.sharding import PartitionSpec as P

HEAD_DIM = 128
QBLOCKS = 4
KBLK = 512


EPSILON = 1e-05
ROPE_BASE = 500000.0
NEGATIVE = -1e30


def swapped(block, axis, apart):
    count = lax.axis_size(axis)
    route = []
    for low in range(count):
        high = low | 1 << apart
        if high != low and high < count:
            route += [(low, high), (high, low)]
    return lax.ppermute(block, axis, route)


def side_by_side(arrays, axis, dim, along):
    both = jnp.concatenate(arrays, axis=along)
    out, at, gathered = (lax.all_gather(both, axis, axis=dim, tiled=True), 0, [])
    for a in arrays:
        gathered.append(lax.slice_in_dim(out, at, at + a.shape[along], axis=along))
        at += a.shape[along]
    return tuple(gathered)


def shifted(value, axis, steps):
    count = lax.axis_size(axis)
    pairs = [(source, (source + steps) % count) for source in range(count)]
    return lax.ppermute(value, axis, pairs)


def rms_scale(row_data, gain):
    floats = row_data.astype(jnp.float32)
    mean_square = jnp.mean(floats * floats, axis=-1, keepdims=True)
    return (floats * lax.rsqrt(mean_square + EPSILON) * gain).astype(jnp.bfloat16)


def doc_layout(doc_lengths, total):
    ends = jnp.cumsum(doc_lengths)
    starts = ends - doc_lengths
    counter = jnp.arange(total, dtype=jnp.int32)
    segment = jnp.sum((counter[:, None] >= ends[None, :-1]).astype(jnp.int32), axis=1)
    labels = jnp.arange(doc_lengths.shape[0], dtype=jnp.int32)
    first = jnp.sum(jnp.where(segment[:, None] == labels[None, :], starts[None, :], 0), axis=1)
    return (segment, counter - first, starts)


def rotate(floats, position):
    half = floats.shape[-1] // 2
    freq = jnp.exp(
        -math.log(ROPE_BASE) * jnp.arange(half, dtype=jnp.float32) * (2.0 / floats.shape[-1])
    )
    angle = position.astype(jnp.float32)[:, None] * freq[None, :]
    cosine = jnp.cos(angle)[:, None, :]
    sine = jnp.sin(angle)[:, None, :]
    lower = floats[..., :half]
    upper = floats[..., half:]
    return jnp.concatenate([lower * cosine - upper * sine, upper * cosine + lower * sine], axis=-1)


def attend(block_query, block_number, key_rows, value_rows, segment, starts, qblk, kblk):
    heads = block_query.shape[1]
    width = block_query.shape[2]
    count = qblk * heads
    flat_query = block_query.reshape(count, width)
    first_row = block_number * qblk
    query_pos = first_row + jnp.arange(qblk, dtype=jnp.int32)
    query_seg = lax.dynamic_slice_in_dim(segment, first_row, qblk)
    pos_rows = jnp.repeat(query_pos, heads)
    seg_rows = jnp.repeat(query_seg, heads)
    labels = jnp.arange(starts.shape[0], dtype=jnp.int32)
    doc_first = jnp.sum(jnp.where(labels == query_seg[0], starts, 0))
    lowest = doc_first // kblk
    highest = (first_row + qblk - 1) // kblk + 1
    factor = 1.0 / math.sqrt(width)

    def advance(key_block, carry):
        peak, totals, summed = carry
        key_start = (key_block * kblk).astype(jnp.int32)
        key_tile = lax.dynamic_slice_in_dim(key_rows, key_start, kblk)
        value_tile = lax.dynamic_slice_in_dim(value_rows, key_start, kblk)
        key_seg = lax.dynamic_slice_in_dim(segment, key_start, kblk)
        key_pos = key_start + jnp.arange(kblk, dtype=jnp.int32)
        scores = (
            lax.dot_general(
                flat_query, key_tile, (((1,), (1,)), ((), ())), preferred_element_type=jnp.float32
            )
            * factor
        )
        allowed = (key_seg[None, :] == seg_rows[:, None]) & (key_pos[None, :] <= pos_rows[:, None])
        scores = jnp.where(allowed, scores, NEGATIVE)
        new_peak = jnp.maximum(peak, jnp.max(scores, axis=1))
        decay = jnp.exp(peak - new_peak)
        weights = jnp.exp(scores - new_peak[:, None])
        totals = totals * decay + jnp.sum(weights, axis=1)
        summed = summed * decay[:, None] + jnp.dot(
            weights.astype(jnp.bfloat16), value_tile, preferred_element_type=jnp.float32
        )
        return (new_peak, totals, summed)

    start_carry = (
        jnp.full((count,), NEGATIVE, jnp.float32),
        jnp.zeros((count,), jnp.float32),
        jnp.zeros((count, width), jnp.float32),
    )
    peak, totals, summed = lax.fori_loop(lowest, highest, advance, start_carry)
    return (summed / totals[:, None]).astype(jnp.bfloat16).reshape(qblk, heads, width)


def body(tokens, doc_lengths, attn_gain, mlp_gain, w_query, w_keyval, w_out, w_gate, w_up, w_down):
    token_count = lax.axis_size("token")
    tensor_count = lax.axis_size("tensor")
    token_index = lax.axis_index("token")
    tensor_index = lax.axis_index("tensor")
    share_rows = tokens.shape[0]
    block_rows = share_rows * tensor_count
    total = block_rows * token_count
    segment, position, starts = doc_layout(doc_lengths, total)
    local_position = lax.dynamic_slice_in_dim(position, token_index * block_rows, block_rows)
    query_cols = w_query.shape[1]
    heads_here = query_cols // HEAD_DIM
    whole_rows = lax.all_gather(tokens, "tensor", axis=0, tiled=True)
    row_data = rms_scale(whole_rows, attn_gain)
    projected = jnp.concatenate(
        [
            jnp.dot(row_data, w_query, preferred_element_type=jnp.float32),
            jnp.dot(row_data, w_keyval, preferred_element_type=jnp.float32),
        ],
        axis=1,
    )
    queries = rotate(
        projected[:, :query_cols].reshape(block_rows, heads_here, HEAD_DIM), local_position
    ).astype(jnp.bfloat16)
    kv_piece = projected[:, query_cols:]
    is_even = tensor_index % 2 == 0
    turned = rotate(kv_piece[:, None, :], local_position)[:, 0]
    own_half = jnp.where(is_even, turned, kv_piece).astype(jnp.bfloat16)
    other_half = swapped(own_half, "tensor", 0)
    keys_local = jnp.where(is_even, own_half, other_half)
    values_local = jnp.where(is_even, other_half, own_half)
    key_rows, value_rows = side_by_side((keys_local, values_local), "token", 0, 1)
    qblk = block_rows // QBLOCKS
    query_blocks = queries.reshape(QBLOCKS, qblk, heads_here, HEAD_DIM)

    def serve(block_query, block_number):
        return attend(block_query, block_number, key_rows, value_rows, segment, starts, qblk, KBLK)

    stride = token_count // QBLOCKS
    answers = [serve(query_blocks[0], token_index * QBLOCKS)]
    for j in range(1, QBLOCKS):
        offset = stride * j
        arrived = shifted(query_blocks[j], "token", offset)
        sender = (token_index - offset) % token_count
        replied = serve(arrived, sender * QBLOCKS + j)
        answers.append(shifted(replied, "token", token_count - offset))
    attn_local = jnp.stack(answers).reshape(block_rows, query_cols)
    partial_sum = jnp.dot(attn_local, w_out, preferred_element_type=jnp.float32)
    summed = lax.psum(partial_sum.astype(jnp.bfloat16), "tensor").astype(jnp.float32)
    state = (whole_rows.astype(jnp.float32) + summed).astype(jnp.bfloat16)
    row_data = rms_scale(state, mlp_gain)
    gate = jnp.dot(row_data, w_gate, preferred_element_type=jnp.float32)
    upward = jnp.dot(row_data, w_up, preferred_element_type=jnp.float32)
    hidden = (jax.nn.silu(gate) * upward).astype(jnp.bfloat16)
    state_share = lax.dynamic_slice_in_dim(state, tensor_index * share_rows, share_rows)
    down = lax.psum_scatter(
        jnp.dot(hidden, w_down, preferred_element_type=jnp.float32).astype(jnp.bfloat16),
        "tensor",
        scatter_dimension=0,
        tiled=True,
    ).astype(jnp.float32)
    return (state_share.astype(jnp.float32) + down).astype(jnp.bfloat16)


def solution(mesh):
    return jax.shard_map(
        body,
        mesh=mesh,
        in_specs=(
            P(("token", "tensor"), None),
            P(),
            P(),
            P(),
            P(None, "tensor"),
            P(None, "tensor"),
            P("tensor", None),
            P(None, "tensor"),
            P(None, "tensor"),
            P("tensor", None),
        ),
        out_specs=P(("token", "tensor"), None),
        check_vma=False,
    )
```

profile of v0, /device:TPU:0, one launch (start us, length us, event | category | flops | bytes accessed | tf_op | source)
XLA Modules:
  0.0 490.8 jit_solution(8948337725778329640)
XLA Ops:
  10.5 3.8 fusion.87
  14.5 68.3 %all-gather.3.cloned.1.call-done = bf16[1024,4096]{1,0:T(8,128)(2,1)} async-done(((bf16[64,4096]{1,0:T(8,128)(2,1)}), bf16[1024,4096]{1,0:T(8,128)(2,1)}) %all-gather.3.cloned.1.call-update) | async-done | bytes 8388624 | tf_op jit(solution)/shard_map/all_gather | solution.py:133
  82.9 5.2 %fusion.59 = f32[1024]{0:T(1024)S(1)} fusion(bf16[1024,4096]{1,0:T(8,128)(2,1)} %all-gather.3.cloned.1.call-done), kind=kLoop, calls=%fused_computation.76 | loop fusion | flops 12581888 | bytes 8392704 | tf_op jit(solution)/shard_map/reduce_sum | solution.py:45
  88.6 4.1 fusion.69
  94.0 1.5 collective-permute-start
  95.5 6.6 %collective-permute-done = bf16[1024,128]{0,1:T(8,128)(2,1)S(1)} collective-permute-done((bf16[1024,128]{0,1:T(8,128)(2,1)S(1)}, bf16[1024,128]{0,1:T(8,128)(2,1)S(1)}, u32[]{:S(2)}, u32[]{:S(2)}) %collective-permute-start) | collective-permute-done | bytes 262176 | tf_op jit(solution)/shard_map/ppermute | solution.py:25
  104.1 6.3 %fusion.67 = f32[1024,256]{0,1:T(8,128)S(1)} fusion(bf16[4096,256]{1,0:T(8,128)(2,1)} %param.22, bf16[1024,4096]{1,0:T(8,128)(2,1)} %all-gather.3.cloned.1.call-done, f32[4096]{0:T(1024)S(1)} %copy-done.4, f32[1024]{0:T(1024)S(1)} %add_rsqrt_fusion.1), kind=kOutput, calls=%fused_computation.84 | convolution fusion | flops 2164260864 | bytes 11554816 | tf_op jit(solution)/shard_map/dot_general | solution.py:137
  110.5 1.6 collective-permute-start.1
  112.1 1.8 collective-permute-start.5
  113.9 1.8 collective-permute-start.3
  126.7 11.5 %all-gather.5.cloned.1.call-done = bf16[8192,256]{0,1:T(8,128)(2,1)} async-done(((bf16[1024,256]{0,1:T(8,128)(2,1)}), bf16[8192,256]{0,1:T(8,128)(2,1)}) %all-gather.5.cloned.1.call-update) | async-done | bytes 4194320 | tf_op jit(solution)/shard_map/all_gather | solution.py:30
  138.1 4.7 fusion.96
  142.8 4.1 copy.37
  146.9 4.1 copy.36
  151.0 20.8 %while.63 = (s32[]{:T(128)}, f32[512]{0:T(512)S(1)}, f32[512]{0:T(512)S(1)}, f32[512,128]{1,0:T(8,128)S(1)}, s32[]{:T(128)}, /*index=5*/s32[8192]{0:T(1024)S(1)}...) while((s32[]{:T(128)}, f32[512]{0:T(512)S(1)}, ...), condition=%wide.region_23.24_spmd.clone, body=%wide.region_20.23_spmd.clone.sunk | while | flops 136971776 | bytes 4124875 | solution.py:117
  155.2 1.3 fusion.155
  171.8 6.9 %while.62 = (s32[]{:T(128)}, f32[512]{0:T(512)S(1)}, f32[512]{0:T(512)S(1)}, f32[512,128]{1,0:T(8,128)S(1)}, s32[]{:T(128)}, /*index=5*/s32[8192]{0:T(1024)S(1)}...) while((s32[]{:T(128)}, f32[512]{0:T(512)S(1)}, ...), condition=%wide.region_18.19_spmd.clone, body=%wide.region_15.18_spmd.clone.sunk | while | flops 136971776 | bytes 4124875 | solution.py:117
  172.4 1.3 fusion.150
  178.8 13.8 %while.61 = (s32[]{:T(128)}, f32[512]{0:T(512)S(1)}, f32[512]{0:T(512)S(1)}, f32[512,128]{1,0:T(8,128)S(1)}, s32[]{:T(128)}, /*index=5*/s32[8192]{0:T(1024)S(1)}...) while((s32[]{:T(128)}, f32[512]{0:T(512)S(1)}, ...), condition=%wide.region_13.14_spmd.clone, body=%wide.region_10.13_spmd.clone.sunk | while | flops 136971776 | bytes 4124875 | solution.py:117
  179.4 1.3 fusion.145
  192.6 3.4 while.60
  196.2 2.3 collective-permute-start.2
  200.0 2.5 collective-permute-done.2
  202.4 2.9 collective-permute-done.4
  207.5 5.6 %convolution_convert_fusion.1 = bf16[1024,4096]{1,0:T(8,128)(2,1)} fusion(bf16[256,4096]{1,0:T(8,128)(2,1)S(1)} %copy-done, bf16[128,8,2,128]{3,2,1,0:T(2,128)(2,1)S(1)} %bitcast.73), kind=kOutput, calls=%fused_computation.81 | convolution fusion | flops 2151677952 | bytes 11010048 | tf_op jit(solution)/shard_map/dot_general | solution.py:168
  213.4 151.7 %all-reduce.2.cloned.1.call-done = bf16[1024,4096]{1,0:T(8,128)(2,1)} async-done(((bf16[1024,4096]{1,0:T(8,128)(2,1)}), bf16[1024,4096]{1,0:T(8,128)(2,1)}) %all-reduce.2.cloned.1.call-update) | async-done | bytes 8388624 | tf_op jit(solution)/shard_map/psum | solution.py:169
  365.2 8.2 %fusion.56 = (f32[1024]{0:T(1024)S(1)}, bf16[1024,4096]{1,0:T(8,128)(2,1)S(1)}) fusion(bf16[1024,4096]{1,0:T(8,128)(2,1)} %all-reduce.2.cloned.1.call-done, bf16[1024,4096]{1,0:T(8,128)(2,1)} %all-gather.3.cloned.1.call-done), kind=kLoop, calls=%fused_computation.73 | loop fusion | flops 29359104 | bytes 25169920 | tf_op jit(solution)/shard_map/reduce_sum | solution.py:45
  373.4 3.2 copy-done.2
  376.6 5.4 %fusion.65 = f32[1024,448]{0,1:T(8,128)} fusion(bf16[4096,448]{0,1:T(8,128)(2,1)S(1)} %copy-done.3, bf16[1024,4096]{1,0:T(8,128)(2,1)S(1)} %get-tuple-element.594, f32[4096]{0:T(1024)S(1)} %copy-done.5, f32[1024]{0:T(1024)S(1)} %add_rsqrt_fusion), kind=kOutput, calls=%fused_computation.83 | convolution fusion | flops 3774873600 | bytes 13914112 | tf_op jit(solution)/shard_map/dot_general | solution.py:172
  382.0 15.8 %convolution_convert_fusion = bf16[1024,4096]{1,0:T(8,128)(2,1)} fusion(bf16[448,4096]{1,0:T(8,128)(2,1)} %param.27, f32[1024,448]{0,1:T(8,128)} %fusion.65, bf16[4096,448]{0,1:T(8,128)(2,1)} %param.26, bf16[1024,4096]{1,0:T(8,128)(2,1)} %copy-done.2, f32[4096]{0:T(1024)S(1)} %copy-done.5, f32[1024]{0:T(1024)S(1)} %add_rsqrt_fusion), kind=kOutput, calls=%fused_computation.80 | convolution fusion | flops 7539916800 | bytes 25972736 | tf_op jit(solution)/shard_map/dot_general | solution.py:177
  397.8 84.4 %reduce-scatter.2.cloned.1.call-done = bf16[64,4096]{1,0:T(8,128)(2,1)} async-done(((bf16[1024,4096]{1,0:T(8,128)(2,1)}), bf16[64,4096]{1,0:T(8,128)(2,1)}) %reduce-scatter.2.cloned.1.call-update) | async-done | bytes 524304 | tf_op jit(solution)/shard_map/reduce_scatter | solution.py:176
  482.2 2.1 add_convert_fusion
  (222 shorter events, 52.4 us)
Async XLA Ops:
  6.5 201.0 %copy-start = (bf16[256,4096]{1,0:T(8,128)(2,1)S(1)}, bf16[256,4096]{1,0:T(8,128)(2,1)}, u32[]{:S(2)}) copy-start(bf16[256,4096]{1,0:T(8,128)(2,1)} %param.24) | copy-start | bytes 6291460
  6.5 81.6 %copy-start.4 = (f32[4096]{0:T(1024)S(1)}, f32[4096]{0:T(1024)}, u32[]{:S(2)}) copy-start(f32[4096]{0:T(1024)} %param.20) | copy-start | bytes 49156
  6.5 76.3 %all-gather.3.cloned.1.call-start = ((), (), s32[]{:S(2)}) async-start(), calls=%async_computation.1 | async-start | bytes 8912896 | tf_op jit(solution)/shard_map/all_gather | solution.py:133
  7.3 130.9 %all-gather.5.cloned.1.call-start = ((), (), s32[]{:S(2)}) async-start(), calls=%async_computation.2 | async-start | bytes 4718592 | tf_op jit(solution)/shard_map/all_gather | solution.py:30
  82.9 5.8 %copy-start.1 = (bf16[1024,4096]{1,0:T(8,128)(2,1)S(1)}, bf16[1024,4096]{1,0:T(8,128)(2,1)}, u32[]{:S(2)}) copy-start(bf16[1024,4096]{1,0:T(8,128)(2,1)} %all-gather.3.cloned.1.call-done) | copy-start | bytes 25165828
  94.0 8.1 %collective-permute-start = (bf16[1024,128]{0,1:T(8,128)(2,1)S(1)}, bf16[1024,128]{0,1:T(8,128)(2,1)S(1)}, u32[]{:S(2)}, u32[]{:S(2)}) collective-permute-start(bf16[1024,128]{0,1:T(8,128)(2,1)S(1)} %fusion.76), channel_id=1, source_target_pairs={{0,1},{1,0},{2,3},{3,2},{4,5},{5,4},{6,7},{7,6},{8,9},{9,8},{10,11... | collective-permute-start | bytes 786440 | tf_op jit(solution)/shard_map/ppermute | solution.py:25
  103.0 262.1 %all-reduce.2.cloned.1.call-start = ((), (), s32[]{:S(2)}) async-start(), calls=%async_computation.3 | async-start | bytes 16777216 | tf_op jit(solution)/shard_map/psum | solution.py:169
  110.5 15.7 %collective-permute-start.1 = (bf16[256,2,128]{0,2,1:T(8,128)(2,1)S(1)}, bf16[256,2,128]{0,2,1:T(8,128)(2,1)S(1)}, u32[]{:S(2)}, u32[]{:S(2)}) collective-permute-start(bf16[256,2,128]{0,2,1:T(8,128)(2,1)S(1)} %get-tuple-element.611), channel_id=1, source_target_pairs={{0,32},{16,48},{32,64},{48,80},{64,96},{80,112},{96,0},{112,16},{1... | collective-permute-start | bytes 393224 | tf_op jit(solution)/shard_map/ppermute | solution.py:40
  112.1 14.3 %collective-permute-start.5 = (bf16[256,2,128]{0,2,1:T(8,128)(2,1)S(1)}, bf16[256,2,128]{0,2,1:T(8,128)(2,1)S(1)}, u32[]{:S(2)}, u32[]{:S(2)}) collective-permute-start(bf16[256,2,128]{0,2,1:T(8,128)(2,1)S(1)} %get-tuple-element.612), channel_id=1, source_target_pairs={{0,96},{16,112},{32,0},{48,16},{64,32},{80,48},{96,64},{112,80},{1... | collective-permute-start | bytes 393224 | tf_op jit(solution)/shard_map/ppermute | solution.py:40
  113.9 12.7 %collective-permute-start.3 = (bf16[256,2,128]{0,2,1:T(8,128)(2,1)S(1)}, bf16[256,2,128]{0,2,1:T(8,128)(2,1)S(1)}, u32[]{:S(2)}, u32[]{:S(2)}) collective-permute-start(bf16[256,2,128]{0,2,1:T(8,128)(2,1)S(1)} %get-tuple-element.613), channel_id=1, source_target_pairs={{0,64},{16,80},{32,96},{48,112},{64,0},{80,16},{96,32},{112,48},{1... | collective-permute-start | bytes 393224 | tf_op jit(solution)/shard_map/ppermute | solution.py:40
  196.2 6.3 %collective-permute-start.2 = (bf16[256,2,128]{2,1,0:T(2,128)(2,1)S(1)}, bf16[256,2,128]{2,1,0:T(2,128)(2,1)S(1)}, u32[]{:S(2)}, u32[]{:S(2)}) collective-permute-start(bf16[256,2,128]{2,1,0:T(2,128)(2,1)S(1)} %bitcast.77), channel_id=1, source_target_pairs={{0,96},{16,112},{32,0},{48,16},{64,32},{80,48},{96,64},{112,80},{1... | collective-permute-start | bytes 393224 | tf_op jit(solution)/shard_map/ppermute | solution.py:40
  198.7 6.7 %collective-permute-start.4 = (bf16[256,2,128]{2,1,0:T(2,128)(2,1)S(1)}, bf16[256,2,128]{2,1,0:T(2,128)(2,1)S(1)}, u32[]{:S(2)}, u32[]{:S(2)}) collective-permute-start(bf16[256,2,128]{2,1,0:T(2,128)(2,1)S(1)} %bitcast.78), channel_id=1, source_target_pairs={{0,64},{16,80},{32,96},{48,112},{64,0},{80,16},{96,32},{112,48},{1... | collective-permute-start | bytes 393224 | tf_op jit(solution)/shard_map/ppermute | solution.py:40
  198.9 7.7 %collective-permute-start.6 = (bf16[256,2,128]{2,1,0:T(2,128)(2,1)S(1)}, bf16[256,2,128]{2,1,0:T(2,128)(2,1)S(1)}, u32[]{:S(2)}, u32[]{:S(2)}) collective-permute-start(bf16[256,2,128]{2,1,0:T(2,128)(2,1)S(1)} %bitcast.79), channel_id=1, source_target_pairs={{0,32},{16,48},{32,64},{48,80},{64,96},{80,112},{96,0},{112,16},{1... | collective-permute-start | bytes 393224 | tf_op jit(solution)/shard_map/ppermute | solution.py:40
  213.1 163.4 %copy-start.5 = (f32[4096]{0:T(1024)S(1)}, f32[4096]{0:T(1024)}, u32[]{:S(2)}) copy-start(f32[4096]{0:T(1024)} %param.21) | copy-start | bytes 49156
  213.1 269.0 %reduce-scatter.2.cloned.1.call-start = ((), (), s32[]{:S(2)}) async-start(), calls=%async_computation.4 | async-start | bytes 8912896 | tf_op jit(solution)/shard_map/reduce_scatter | solution.py:176
  365.2 11.4 %copy-start.3 = (bf16[4096,448]{0,1:T(8,128)(2,1)S(1)}, bf16[4096,448]{0,1:T(8,128)(2,1)}, u32[]{:S(2)}) copy-start(bf16[4096,448]{0,1:T(8,128)(2,1)} %param.25) | copy-start | bytes 11010052
  373.3 3.2 copy-start.2
Sparse Core Ops, SparseCore 0:
  9.5 73.3 all-gather.2
  103.1 34.9 all-gather.4
  213.2 151.8 all-reduce.1
  397.9 84.1 reduce-scatter.1
where the time goes:
time: 494 us; the launch traced here: 491 us
  waiting for transfers between devices  330 us (67%)
  matrix products  70.8 us (14%)
  other arithmetic  28.3 us (6%)
  local copies, waits for them, and re-layouts  26.3 us (5%)
  between operations  24 us (5%)
  starting transfers between devices  10.3 us (2%)
    psum x1, waiting for transfers between devices, body(): lax.psum(partial_sum.astype(jnp.bfloat16), 'tensor').astype(jnp.float32)  152 us
    reduce_scatter x1, waiting for transfers between devices, body(): lax.psum_scatter(jnp.dot(hidden, w_down, preferred_element_type=jnp.float...  84.4 us
    all_gather x1, waiting for transfers between devices, body(): whole_rows = lax.all_gather(tokens, 'tensor', axis=0, tiled=True)  68.3 us
    dot_general x13, matrix products, advance(): lax.dot_general(flat_query, key_tile, (((1,), (1,)), ((), ())), preferred...  16.9 us
    dot_general x13, matrix products, advance(): jnp.dot(weights.astype(jnp.bfloat16), value_tile, preferred_element_type=...  16.8 us
    dot_general x1, matrix products, body(): jnp.dot(hidden, w_down, preferred_element_type=jnp.float32)  15.8 us
    reduce_sum x2, other arithmetic, rms_scale(): mean_square = jnp.mean(floats * floats, axis=-1, keepdims=True)  13.4 us
    unnamed x14, local copies, waits for them, and re-layouts  11.9 us
  transfers between devices with their start and end apart: 11, of which 8 were waited for; matrix products, arithmetic and copies ran while one was open for 3% of the time, Pallas kernels for 0%

commit v1 on v0

v1 whole, which is shorter than its diff:
```python
import functools
import math

import jax
import jax.numpy as jnp
from jax import lax
from jax.experimental import pallas as pl
from jax.experimental.pallas import tpu as pltpu
from jax.sharding import PartitionSpec as P

HEAD_DIM = 128
KBLK = 512
SIDE = 4

EPSILON = 1e-05
ROPE_BASE = 500000.0
NEGATIVE = -1e30
MESH = pl.DeviceIdType.MESH

RANK = {0: 0, 3: 1, 1: 2, 2: 3}
ARRIVE = (0, 3, 1, 2)
DEPART = (2, 1, 3, 0)


def neighbour(half, first, step):
    me = lax.axis_index("tensor")
    z, x = me // SIDE, me % SIDE
    if (half == 0) == first:
        x = (x + step + SIDE) % SIDE
    else:
        z = (z + step + SIDE) % SIDE
    return {"tensor": z * SIDE + x}


def block_number(dz, dx):
    me = lax.axis_index("tensor")
    z, x = me // SIDE, me % SIDE
    return ((z + dz) % SIDE) * SIDE + (x + dx) % SIDE


def offsets(half, s, f):
    return (s, f) if half == 0 else (f, s)


def greet():
    barrier = pltpu.get_barrier_semaphore()
    for first in (True, False):
        for step in (1, -1):
            pl.semaphore_signal(barrier, inc=1, device_id=neighbour(0, first, step), device_id_type=MESH)
    pl.semaphore_wait(barrier, 4)


class Wires:
    def __init__(self, send_sems, recv_sems):
        self.send_sems, self.recv_sems, self.slots, self.started = send_sems, recv_sems, {}, []

    def copy(self, key, src, dst, device):
        slot = self.slots.setdefault(key, len(self.slots))
        return pltpu.make_async_remote_copy(
            src_ref=src,
            dst_ref=dst,
            send_sem=self.send_sems.at[slot],
            recv_sem=self.recv_sems.at[slot],
            device_id=device,
            device_id_type=MESH,
        )

    def start(self, key, src, dst, device):
        made = self.copy(key, src, dst, device)
        made.start()
        self.started.append(made)

    def arrive(self, key, dst, device):
        self.copy(key, dst, dst, device).wait_recv()

    def drain(self):
        for made in self.started:
            made.wait_send()
        self.started = []


def gather(wires, blocks, halves, consume):
    rows = blocks.shape[3]
    low, high = pl.ds(0, rows // 2), pl.ds(rows // 2, rows // 2)

    def at(h, s, f, part=None):
        return blocks.at[h, s, f] if part is None else blocks.at[h, s, f, part]

    def spread(h, f):
        wires.start((h, "s", 3, f), at(h, 0, f), at(h, 3, f), neighbour(h, False, 1))
        wires.start((h, "s", 1, f), at(h, 0, f), at(h, 1, f), neighbour(h, False, -1))

    def relay_second(h, f):
        wires.arrive((h, "s", 3, f), at(h, 3, f), neighbour(h, False, -1))
        wires.start((h, "t", 0, f), at(h, 3, f, low), at(h, 2, f, low), neighbour(h, False, 1))
        wires.arrive((h, "s", 1, f), at(h, 1, f), neighbour(h, False, 1))
        wires.start((h, "t", 1, f), at(h, 1, f, high), at(h, 2, f, high), neighbour(h, False, -1))

    for h in halves:
        wires.start((h, "f", 3), at(h, 0, 0), at(h, 0, 3), neighbour(h, True, 1))
        wires.start((h, "f", 1), at(h, 0, 0), at(h, 0, 1), neighbour(h, True, -1))
    for h in halves:
        spread(h, 0)
    for h in halves:
        wires.arrive((h, "f", 3), at(h, 0, 3), neighbour(h, True, -1))
        wires.start((h, "g", 0), at(h, 0, 3, low), at(h, 0, 2, low), neighbour(h, True, 1))
        wires.arrive((h, "f", 1), at(h, 0, 1), neighbour(h, True, 1))
        wires.start((h, "g", 1), at(h, 0, 1, high), at(h, 0, 2, high), neighbour(h, True, -1))
    for h in halves:
        spread(h, 3)
        spread(h, 1)
    for h in halves:
        relay_second(h, 0)
    for h in halves:
        wires.arrive((h, "g", 0), at(h, 0, 2, low), neighbour(h, True, -1))
        wires.arrive((h, "g", 1), at(h, 0, 2, high), neighbour(h, True, 1))
        spread(h, 2)
    for h in halves:
        consume(h, 0)
    for f in (3, 1, 2):
        for h in halves:
            relay_second(h, f)
    for s in (3, 1):
        for h in halves:
            consume(h, s)
    for h in halves:
        for f in (0, 3, 1, 2):
            wires.arrive((h, "t", 0, f), at(h, 2, f, low), neighbour(h, False, -1))
            wires.arrive((h, "t", 1, f), at(h, 2, f, high), neighbour(h, False, 1))
        consume(h, 2)
    wires.drain()


def scatter(wires, out, half_in, full_in, edge_half, edge_full, halves, produce):
    rows = out.shape[3]
    low, high = pl.ds(0, rows // 2), pl.ds(rows // 2, rows // 2)
    f32 = jnp.float32

    def wide(ref):
        return ref[...].astype(f32)

    for h in halves:
        produce(h, 2)
        for f in DEPART:
            wires.start((h, "a", 0, f), out.at[h, 2, f, low], half_in.at[h, 0, f], neighbour(h, False, 1))
            wires.start((h, "a", 1, f), out.at[h, 2, f, high], half_in.at[h, 1, f], neighbour(h, False, -1))
    for h in halves:
        produce(h, 1)
        produce(h, 3)
    for f in DEPART:
        for h in halves:
            wires.arrive((h, "a", 0, f), half_in.at[h, 0, f], neighbour(h, False, -1))
            mine = out.at[h, 1, f, low]
            mine[...] = (wide(mine) + wide(half_in.at[h, 0, f])).astype(mine.dtype)
            wires.start((h, "b", 0, f), out.at[h, 1, f], full_in.at[h, 0, f], neighbour(h, False, 1))
            wires.arrive((h, "a", 1, f), half_in.at[h, 1, f], neighbour(h, False, 1))
            mine = out.at[h, 3, f, high]
            mine[...] = (wide(mine) + wide(half_in.at[h, 1, f])).astype(mine.dtype)
            wires.start((h, "b", 1, f), out.at[h, 3, f], full_in.at[h, 1, f], neighbour(h, False, -1))
    for h in halves:
        produce(h, 0)

    def settle(h, f):
        wires.arrive((h, "b", 0, f), full_in.at[h, 0, f], neighbour(h, False, -1))
        wires.arrive((h, "b", 1, f), full_in.at[h, 1, f], neighbour(h, False, 1))
        return wide(out.at[h, 0, f]) + wide(full_in.at[h, 0, f]) + wide(full_in.at[h, 1, f])

    for h in halves:
        mine = out.at[h, 0, 2]
        mine[...] = settle(h, 2).astype(mine.dtype)
        wires.start((h, "c", 0), out.at[h, 0, 2, low], edge_half.at[h, 0], neighbour(h, True, 1))
        wires.start((h, "c", 1), out.at[h, 0, 2, high], edge_half.at[h, 1], neighbour(h, True, -1))
    for h in halves:
        for way, f, part, step in ((0, 1, low, 1), (1, 3, high, -1)):
            mine = out.at[h, 0, f]
            mine[...] = settle(h, f).astype(mine.dtype)
            wires.arrive((h, "c", way), edge_half.at[h, way], neighbour(h, True, -step))
            mine = out.at[h, 0, f, part]
            mine[...] = (wide(mine) + wide(edge_half.at[h, way])).astype(mine.dtype)
            wires.start((h, "d", way), out.at[h, 0, f], edge_full.at[h, way], neighbour(h, True, step))
    total = {}
    for h in halves:
        own = settle(h, 0)
        wires.arrive((h, "d", 0), edge_full.at[h, 0], neighbour(h, True, -1))
        wires.arrive((h, "d", 1), edge_full.at[h, 1], neighbour(h, True, 1))
        total[h] = own + wide(edge_full.at[h, 0]) + wide(edge_full.at[h, 1])
    wires.drain()
    return total


def norm_halves(rows, gain, width):
    mean_square = jnp.mean(rows * rows, axis=-1, keepdims=True)
    normed = (rows * lax.rsqrt(mean_square + EPSILON) * gain).astype(jnp.bfloat16)
    return normed[:, :width], normed[:, width:]


def project_kernel(
    tokens_ref, gain_ref, cos_ref, sin_ref, wq_hbm, wkv_hbm, q_ref, kv_ref,
    weights, blocks, acc, load_sems, send_sems, recv_sems,
):
    half_width = blocks.shape[4]
    qcols = wq_hbm.shape[1]
    cols = qcols + wkv_hbm.shape[1]
    loads = [
        pltpu.make_async_copy(wq_hbm, weights.at[:, pl.ds(0, qcols)], load_sems.at[0]),
        pltpu.make_async_copy(wkv_hbm, weights.at[:, pl.ds(qcols, cols - qcols)], load_sems.at[1]),
    ]
    for load in loads:
        load.start()
    greet()
    first, second = norm_halves(tokens_ref[...].astype(jnp.float32), gain_ref[...], half_width)
    blocks[0, 0, 0] = first
    blocks[1, 0, 0] = second
    holds_keys = lax.axis_index("tensor") % 2 == 0
    loaded = []

    def consume(h, s):
        if not loaded:
            for load in loads:
                load.wait()
            loaded.append(True)
        rows = blocks.shape[3]
        left = blocks[h, s].reshape(SIDE * rows, half_width)
        part = jnp.dot(
            left, weights[h * half_width : (h + 1) * half_width, :], preferred_element_type=jnp.float32
        ).reshape(SIDE, rows, cols)
        for f in range(SIDE):
            dz, dx = offsets(h, s, f)
            earlier = RANK[f] < RANK[s] or (RANK[f] == RANK[s] and h == 1)
            if not earlier:
                acc[dz, dx] = part[f]
                continue
            whole = acc[dz, dx] + part[f]
            number = block_number(dz, dx)
            cosine, sine = cos_ref[number], sin_ref[number]
            for head in range(qcols // HEAD_DIM):
                piece = whole[:, head * HEAD_DIM : (head + 1) * HEAD_DIM]
                turned = piece * cosine + pltpu.roll(piece, HEAD_DIM // 2, 1) * sine
                q_ref[number, :, head * HEAD_DIM : (head + 1) * HEAD_DIM] = turned.astype(jnp.bfloat16)
            piece = whole[:, qcols:]
            turned = piece * cosine + pltpu.roll(piece, HEAD_DIM // 2, 1) * sine
            kv_ref[number] = jnp.where(holds_keys, turned, piece).astype(jnp.bfloat16)

    gather(Wires(send_sems, recv_sems), blocks, (0, 1), consume)


def project(tokens, gain, cosine, sine, w_query, w_keyval):
    rows, width = tokens.shape
    devices = SIDE * SIDE
    cols = w_query.shape[1] + w_keyval.shape[1]
    vmem = pl.BlockSpec(memory_space=pltpu.VMEM)
    hbm = pl.BlockSpec(memory_space=pl.ANY)
    return pl.pallas_call(
        project_kernel,
        out_shape=(
            jax.ShapeDtypeStruct((devices, rows, w_query.shape[1]), jnp.bfloat16),
            jax.ShapeDtypeStruct((devices, rows, w_keyval.shape[1]), jnp.bfloat16),
        ),
        in_specs=[vmem] * 4 + [hbm] * 2,
        out_specs=(vmem, vmem),
        scratch_shapes=[
            pltpu.VMEM((width, cols), jnp.bfloat16),
            pltpu.VMEM((2, SIDE, SIDE, rows, width // 2), jnp.bfloat16),
            pltpu.VMEM((SIDE, SIDE, rows, cols), jnp.float32),
            pltpu.SemaphoreType.DMA((2,)),
            pltpu.SemaphoreType.DMA((40,)),
            pltpu.SemaphoreType.DMA((40,)),
        ],
        compiler_params=pltpu.CompilerParams(
            collective_id=0, has_side_effects=True, vmem_limit_bytes=40 << 20
        ),
        name="project",
    )(tokens, gain, cosine, sine, w_query, w_keyval)


def finish_kernel(
    tokens_ref, attn_ref, gain_ref, wo_hbm, wg_hbm, wu_hbm, wd_hbm, out_ref,
    wo, wg, wu, wd, blocks, acc_gate, acc_up, hidden, sending, half_in, full_in, edge_half, edge_full, state,
    load_sems, send_sems, recv_sems,
):
    rows, half_width = blocks.shape[3], blocks.shape[4]
    loads = [
        pltpu.make_async_copy(src, dst, load_sems.at[i])
        for i, (src, dst) in enumerate(((wo_hbm, wo), (wg_hbm, wg), (wu_hbm, wu), (wd_hbm, wd)))
    ]
    for load in loads:
        load.start()
    greet()
    halves = (0, 1)
    loads[0].wait()

    def columns(h):
        return pl.ds(h * half_width, half_width)

    def project_out(h, s):
        left = jnp.concatenate([attn_ref[block_number(*offsets(h, s, f))] for f in range(SIDE)], axis=0)
        part = jnp.dot(left, wo[:, columns(h)], preferred_element_type=jnp.float32)
        sending[h, s] = part.astype(jnp.bfloat16).reshape(SIDE, rows, half_width)

    proj = scatter(
        Wires(send_sems.at[0], recv_sems.at[0]),
        sending, half_in, full_in, edge_half, edge_full, halves, project_out,
    )
    for h in halves:
        state[:, columns(h)] = (tokens_ref[:, columns(h)].astype(jnp.float32) + proj[h]).astype(jnp.bfloat16)
    first, second = norm_halves(state[...].astype(jnp.float32), gain_ref[...], half_width)
    blocks[0, 0, 0] = first
    blocks[1, 0, 0] = second
    loads[1].wait()
    loads[2].wait()

    def gated(h, s):
        left = blocks[h, s].reshape(SIDE * rows, half_width)
        gate = jnp.dot(left, wg[columns(h), :], preferred_element_type=jnp.float32)
        upward = jnp.dot(left, wu[columns(h), :], preferred_element_type=jnp.float32)
        for f in range(SIDE):
            dz, dx = offsets(h, s, f)
            earlier = RANK[f] < RANK[s] or (RANK[f] == RANK[s] and h == 1)
            g, u = gate[f * rows : (f + 1) * rows], upward[f * rows : (f + 1) * rows]
            if not earlier:
                acc_gate[dz, dx], acc_up[dz, dx] = g, u
                continue
            g, u = g + acc_gate[dz, dx], u + acc_up[dz, dx]
            hidden[dz, dx] = (g / (1.0 + jnp.exp(-g)) * u).astype(jnp.bfloat16)

    gather(Wires(send_sems.at[1], recv_sems.at[1]), blocks, halves, gated)
    loads[3].wait()

    def project_down(h, s):
        left = jnp.concatenate([hidden[offsets(h, s, f)] for f in range(SIDE)], axis=0)
        part = jnp.dot(left, wd[:, columns(h)], preferred_element_type=jnp.float32)
        sending[h, s] = part.astype(jnp.bfloat16).reshape(SIDE, rows, half_width)

    down = scatter(
        Wires(send_sems.at[2], recv_sems.at[2]),
        sending, half_in, full_in, edge_half, edge_full, halves, project_down,
    )
    for h in halves:
        out_ref[:, columns(h)] = (state[:, columns(h)].astype(jnp.float32) + down[h]).astype(jnp.bfloat16)


def finish(tokens, attn, gain, w_out, w_gate, w_up, w_down):
    rows, width = tokens.shape
    hidden = w_gate.shape[1]
    vmem = pl.BlockSpec(memory_space=pltpu.VMEM)
    hbm = pl.BlockSpec(memory_space=pl.ANY)
    half = width // 2
    bf16 = jnp.bfloat16
    return pl.pallas_call(
        finish_kernel,
        out_shape=jax.ShapeDtypeStruct((rows, width), bf16),
        in_specs=[vmem] * 3 + [hbm] * 4,
        out_specs=vmem,
        scratch_shapes=[
            pltpu.VMEM(w_out.shape, bf16),
            pltpu.VMEM(w_gate.shape, bf16),
            pltpu.VMEM(w_up.shape, bf16),
            pltpu.VMEM(w_down.shape, bf16),
            pltpu.VMEM((2, SIDE, SIDE, rows, half), bf16),
            pltpu.VMEM((SIDE, SIDE, rows, hidden), jnp.float32),
            pltpu.VMEM((SIDE, SIDE, rows, hidden), jnp.float32),
            pltpu.VMEM((SIDE, SIDE, rows, hidden), bf16),
            pltpu.VMEM((2, SIDE, SIDE, rows, half), bf16),
            pltpu.VMEM((2, 2, SIDE, rows // 2, half), bf16),
            pltpu.VMEM((2, 2, SIDE, rows, half), bf16),
            pltpu.VMEM((2, 2, rows // 2, half), bf16),
            pltpu.VMEM((2, 2, rows, half), bf16),
            pltpu.VMEM((rows, width), bf16),
            pltpu.SemaphoreType.DMA((4,)),
            pltpu.SemaphoreType.DMA((3, 40)),
            pltpu.SemaphoreType.DMA((3, 40)),
        ],
        compiler_params=pltpu.CompilerParams(
            collective_id=1, has_side_effects=True, vmem_limit_bytes=60 << 20
        ),
        name="finish",
    )(tokens, attn, gain, w_out, w_gate, w_up, w_down)


def attend_kernel(bounds, q_ref, k_ref, v_ref, first_ref, o_ref, *, qblk):
    block = pl.program_id(0)
    low, high, clear_low, clear_high, row0 = (bounds[i, block] for i in range(5))
    heads = q_ref.shape[1] // HEAD_DIM
    rows = heads * qblk
    factor = math.log2(math.e) / math.sqrt(HEAD_DIM)
    query = jnp.concatenate([q_ref[:, h * HEAD_DIM : (h + 1) * HEAD_DIM] for h in range(heads)], axis=0)
    first = jnp.concatenate([first_ref[...]] * heads, axis=0)
    spot = lax.broadcasted_iota(jnp.int32, (qblk, 1), 0) + row0
    last = jnp.concatenate([spot] * heads, axis=0)

    def advance(masked, number, carry):
        peak, totals, summed = carry
        start = pl.multiple_of(number * KBLK, KBLK)
        keys = k_ref[pl.ds(start, KBLK), :]
        values = v_ref[pl.ds(start, KBLK), :]
        scores = lax.dot_general(query, keys, (((1,), (1,)), ((), ())), preferred_element_type=jnp.float32) * factor
        if masked:
            spots = lax.broadcasted_iota(jnp.int32, (rows, KBLK), 1) + start
            scores = jnp.where((spots >= first) & (spots <= last), scores, NEGATIVE)
        new_peak = jnp.maximum(peak, jnp.max(scores, axis=1, keepdims=True))
        decay = jnp.exp2(peak - new_peak)
        weights = jnp.exp2(scores - new_peak)
        totals = totals * decay + jnp.sum(weights, axis=1, keepdims=True)
        summed = summed * decay + jnp.dot(weights.astype(jnp.bfloat16), values, preferred_element_type=jnp.float32)
        return new_peak, totals, summed

    carry = (
        jnp.full((rows, 1), NEGATIVE, jnp.float32),
        jnp.zeros((rows, 1), jnp.float32),
        jnp.zeros((rows, HEAD_DIM), jnp.float32),
    )
    carry = lax.fori_loop(low, clear_low, functools.partial(advance, True), carry)
    carry = lax.fori_loop(clear_low, clear_high, functools.partial(advance, False), carry)
    peak, totals, summed = lax.fori_loop(clear_high, high, functools.partial(advance, True), carry)
    answer = (summed / totals).astype(jnp.bfloat16)
    for h in range(heads):
        o_ref[:, h * HEAD_DIM : (h + 1) * HEAD_DIM] = answer[h * qblk : (h + 1) * qblk]


def attend(queries, keys, values, first, bounds, qblk):
    total, cols = queries.shape
    whole = pl.BlockSpec(memory_space=pltpu.VMEM)
    return pl.pallas_call(
        functools.partial(attend_kernel, qblk=qblk),
        out_shape=jax.ShapeDtypeStruct((total, cols), jnp.bfloat16),
        grid_spec=pltpu.PrefetchScalarGridSpec(
            num_scalar_prefetch=1,
            grid=(total // qblk,),
            in_specs=[
                pl.BlockSpec((qblk, cols), lambda i, b: (i, 0)),
                whole,
                whole,
                pl.BlockSpec((qblk, 1), lambda i, b: (i, 0)),
            ],
            out_specs=pl.BlockSpec((qblk, cols), lambda i, b: (i, 0)),
        ),
        compiler_params=pltpu.CompilerParams(vmem_limit_bytes=40 << 20),
        name="attend",
    )(bounds, queries, keys, values, first)


def swapped(block, axis):
    count = lax.axis_size(axis)
    return lax.ppermute(block, axis, [(i, i ^ 1) for i in range(count)])


def body(tokens, doc_lengths, attn_gain, mlp_gain, w_query, w_keyval, w_out, w_gate, w_up, w_down):
    devices = lax.axis_size("tensor")
    token_index = lax.axis_index("token")
    tensor_index = lax.axis_index("tensor")
    rows = tokens.shape[0]
    block_rows = rows * devices
    ends = jnp.cumsum(doc_lengths)
    spots = token_index * block_rows + jnp.arange(block_rows, dtype=jnp.int32)
    passed = spots[:, None] >= ends[None, :-1]
    first = jnp.max(jnp.where(passed, ends[None, :-1], 0), axis=1)
    position = (spots - first).astype(jnp.float32)
    half = HEAD_DIM // 2
    freq = jnp.exp(-math.log(ROPE_BASE) * jnp.arange(half, dtype=jnp.float32) * (2.0 / HEAD_DIM))
    angle = position[:, None] * freq[None, :]
    cosine, sine = jnp.cos(angle), jnp.sin(angle)
    cosine = jnp.concatenate([cosine, cosine], axis=1).reshape(devices, rows, HEAD_DIM)
    sine = jnp.concatenate([-sine, sine], axis=1).reshape(devices, rows, HEAD_DIM)
    queries, own_half = project(tokens, attn_gain[None, :], cosine, sine, w_query, w_keyval)
    queries = queries.reshape(block_rows, w_query.shape[1])
    own_half = own_half.reshape(block_rows, HEAD_DIM)
    is_even = tensor_index % 2 == 0
    other_half = swapped(own_half, "tensor")
    keys = jnp.where(is_even, own_half, other_half)
    values = jnp.where(is_even, other_half, own_half)
    both = lax.all_gather(jnp.concatenate([keys, values], axis=1), "token", axis=0, tiled=True)
    qblk = 256
    heads_of = first[::qblk]
    tails_of = first[qblk - 1 :: qblk]
    row0 = spots[::qblk]
    low = heads_of // KBLK
    high = (row0 + qblk - 1) // KBLK + 1
    clear_low = jnp.minimum((tails_of + KBLK - 1) // KBLK, high)
    clear_high = jnp.maximum(row0 // KBLK, clear_low)
    bounds = jnp.stack([low, high, clear_low, clear_high, row0]).astype(jnp.int32)
    attn = attend(queries, both[:, :HEAD_DIM], both[:, HEAD_DIM:], first[:, None].astype(jnp.int32), bounds, qblk)
    attn = attn.reshape(devices, rows, attn.shape[1])
    return finish(tokens, attn, mlp_gain[None, :], w_out, w_gate, w_up, w_down)


def solution(mesh):
    return jax.shard_map(
        body,
        mesh=mesh,
        in_specs=(
            P(("token", "tensor"), None),
            P(),
            P(),
            P(),
            P(None, "tensor"),
            P(None, "tensor"),
            P("tensor", None),
            P(None, "tensor"),
            P(None, "tensor"),
            P("tensor", None),
        ),
        out_specs=P(("token", "tensor"), None),
        check_vma=False,
    )
```

time: 494 us -> 276 us (0.56)
  the two profiles are of different devices: /device:TPU:0 before, /device:TPU:9 now
where the time goes in v1:
time: 276 us
  Pallas kernels  214 us (78%)
  waiting for transfers between devices  25 us (9%)
  local copies, waits for them, and re-layouts  18.7 us (7%)
  between operations  13.5 us (5%)
  other arithmetic  4.26 us (2%)
    pallas_call x1, Pallas kernels, finish(): pl.pallas_call(finish_kernel, out_shape=jax.ShapeDtypeStruct((rows, width...  140 us
    pallas_call x1, Pallas kernels, project(): pl.pallas_call(project_kernel, out_shape=(jax.ShapeDtypeStruct((devices,...  51.5 us
    pallas_call x1, Pallas kernels, attend(): pl.pallas_call(functools.partial(attend_kernel, qblk=qblk), out_shape=jax...  22.4 us
    all_gather x1, waiting for transfers between devices, body(): lax.all_gather(jnp.concatenate([keys, values], axis=1), 'token', axis=0,...  18.7 us
    unnamed x13, local copies, waits for them, and re-layouts  15.6 us
    ppermute x1, waiting for transfers between devices, swapped(): return lax.ppermute(block, axis, [(i, i ^ 1) for i in range(count)])  6.23 us
  transfers between devices with their start and end apart: 2, of which 2 were waited for; matrix products, arithmetic and copies ran while one was open for 5% of the time, Pallas kernels for 0%

profile of v1, /device:TPU:9, one launch (start us, length us, event | category | flops | bytes accessed | tf_op | source)
XLA Modules:
  0.0 275.8 jit_solution(7868663182671509061)
XLA Ops:
  6.5 0.0 copy-start.4
  6.5 0.0 copy-start
  6.5 0.0 all-gather.2.cloned.1.call-start
  6.6 1.0 reduce-window.4
  7.6 0.1 select_reduce_fusion
  7.6 0.1 reduce_max.14
  7.7 0.0 copy-start.3
  7.7 1.9 fusion
  9.6 0.3 pad_maximum_fusion
  10.0 0.0 copy-done.4
  10.0 0.0 copy-done
  10.0 0.0 copy-done.2
  10.0 0.0 copy-done.3
  10.0 51.5 %project.1 = (bf16[16,64,256]{2,1,0:T(8,128)(2,1)S(1)}, bf16[16,64,128]{2,1,0:T(8,128)(2,1)S(1)}) custom-call(bf16[64,4096]{1,0:T(8,128)(2,1)S(1)} %copy-done, f32[1,4096]{1,0:T(1,128)S(1)} %bitcast.21, f32[16,64,128]{2,1,0:T(8,128)S(1)} %get-tuple-element.19.cos_ref, f32[16,64,128]{2,1,0:T(8,128)S(1)} %get-tuple-element.20.sin_ref, ...), custom_call_target="tpu_custom_call" | custom-call | tf_op jit(solution)/shard_map/project/pallas_call | solution.py:253
  61.6 0.3 collective-permute-start
  61.9 6.2 %collective-permute-done = bf16[1024,128]{1,0:T(8,128)(2,1)S(1)} collective-permute-done((bf16[1024,128]{1,0:T(8,128)(2,1)S(1)}, bf16[1024,128]{1,0:T(8,128)(2,1)S(1)}, u32[]{:S(2)}, u32[]{:S(2)}) %collective-permute-start) | collective-permute-done | bytes 262176 | tf_op jit(solution)/shard_map/ppermute | solution.py:444
  68.1 0.1 broadcast_select_fusion.1
  68.1 0.9 pad_maximum_fusion.2
  69.0 0.0 all-gather.2.cloned.1.call-update
  69.0 0.1 slice.23
  69.1 0.1 slice.22
  69.2 0.1 slice.21
  69.3 0.2 copy.16.first_ref
  69.5 6.4 %copy.17.wg_hbm = bf16[4096,448]{1,0:T(8,128)(2,1)} copy(bf16[4096,448]{0,1:T(8,128)(2,1)} %param.17) | data formatting | bytes 7340032 | tf_op args[7]
  75.9 6.5 %copy.18.wu_hbm = bf16[4096,448]{1,0:T(8,128)(2,1)} copy(bf16[4096,448]{0,1:T(8,128)(2,1)} %param.18) | data formatting | bytes 7340032 | tf_op args[8]
  82.5 18.7 %all-gather.2.cloned.1.call-done = bf16[8192,256]{1,0:T(8,128)(2,1)} async-done(((bf16[1024,256]{1,0:T(8,128)(2,1)}), bf16[8192,256]{1,0:T(8,128)(2,1)}) %all-gather.2.cloned.1.call-update) | async-done | bytes 4194320 | tf_op jit(solution)/shard_map/all_gather | solution.py:471
  101.2 2.5 fusion.6
  103.7 22.4 %attend.1 = bf16[1024,256]{1,0:T(8,128)(2,1)S(1)} custom-call(s32[5,4]{1,0:T(8,128)S(1)} %stack.23.bounds, bf16[1024,256]{1,0:T(8,128)(2,1)S(1)} %bitcast.19, bf16[8192,128]{1,0:T(8,128)(2,1)S(1)} %get-tuple-element.13.k_ref, bf16[8192,128]{1,0:T(8,128)(2,1)S(1)} %get-tuple-element.12.v_ref, s32[1024,1]{1,0:T(8,128)S(1)} %copy.16.first_ref), custom_call_target="tpu_custom_call" | custom-call | tf_op jit(solution)/shard_map/attend/pallas_call | solution.py:423
  126.1 0.0 copy-start.1
  126.1 0.8 copy-done.1
  126.9 140.2 %finish.1 = bf16[64,4096]{1,0:T(8,128)(2,1)} custom-call(bf16[64,4096]{1,0:T(8,128)(2,1)} %tokens_ref.3, bf16[16,64,256]{2,1,0:T(8,128)(2,1)} %bitcast.18, f32[1,4096]{1,0:T(1,128)} %bitcast.23, bf16[256,4096]{1,0:T(8,128)(2,1)} %wo_hbm.1, bf16[4096,448]{1,0:T(8,128)(2,1)} %copy.17.wg_hbm, bf16[4096,448]{1,0:T(8,128)(2,1)} %copy.18.wu_hbm, ...), custom_call_target="tpu_custom_call" | custom-call | tf_op jit(solution)/shard_map/finish/pallas_call | solution.py:349
  267.1 1.9 copy.20
  (8 shorter events, 0.1 us)
Async XLA Ops:
  6.5 3.4 %copy-start.4 = (f32[4096]{0:T(1024)S(1)}, f32[4096]{0:T(1024)}, u32[]{:S(2)}) copy-start(f32[4096]{0:T(1024)} %param.12) | copy-start | bytes 49156
  6.5 3.5 %copy-start = (bf16[64,4096]{1,0:T(8,128)(2,1)S(1)}, bf16[64,4096]{1,0:T(8,128)(2,1)}, u32[]{:S(2)}) copy-start(bf16[64,4096]{1,0:T(8,128)(2,1)} %tokens_ref.3) | copy-start | bytes 1572868
  6.5 3.5 %copy-start.2 = (bf16[4096,256]{1,0:T(8,128)(2,1)S(1)}, bf16[4096,256]{1,0:T(8,128)(2,1)}, u32[]{:S(2)}) copy-start(bf16[4096,256]{1,0:T(8,128)(2,1)} %wq_hbm.1) | copy-start | bytes 6291460
  6.5 94.7 %all-gather.2.cloned.1.call-start = ((), (), s32[]{:S(2)}) async-start(), calls=%async_computation | async-start | bytes 4718592 | tf_op jit(solution)/shard_map/all_gather | solution.py:471
  7.7 2.3 copy-start.3
  61.6 6.5 %collective-permute-start = (bf16[1024,128]{1,0:T(8,128)(2,1)S(1)}, bf16[1024,128]{1,0:T(8,128)(2,1)S(1)}, u32[]{:S(2)}, u32[]{:S(2)}) collective-permute-start(bf16[1024,128]{1,0:T(8,128)(2,1)S(1)} %bitcast.20), channel_id=1, source_target_pairs={{0,1},{1,0},{2,3},{3,2},{4,5},{5,4},{6,7},{7,6},{8,9},{9,8},{10,11... | collective-permute-start | bytes 786440 | tf_op jit(solution)/shard_map/ppermute | solution.py:444
  126.1 0.8 copy-start.1
Sparse Core Ops, SparseCore 0:
  69.1 32.0 all-gather.1

commit v2 on v1

v2 whole, which is shorter than its diff:
```python
import functools
import math

import jax
import jax.numpy as jnp
from jax import lax
from jax.experimental import pallas as pl
from jax.experimental.pallas import tpu as pltpu
from jax.sharding import PartitionSpec as P

HEAD_DIM = 128
KBLK = 512
SIDE = 4
CORES = 2
YS = 4

EPSILON = 1e-05
ROPE_BASE = 500000.0
NEGATIVE = -1e30
MESH = pl.DeviceIdType.MESH


def place():
    me, token = lax.axis_index("tensor"), lax.axis_index("token")
    return me // SIDE, me % SIDE, token // CORES, token % CORES


def along_z(step):
    z, x, _, _ = place()
    return {"tensor": ((z + step + SIDE) % SIDE) * SIDE + x}


def mate():
    z, x, _, _ = place()
    return {"tensor": z * SIDE + SIDE - 1 - x}


def holder():
    z, x, _, _ = place()
    return {"tensor": z * SIDE + x + 1 - 2 * (x % 2)}


def along_y(step):
    _, _, y, core = place()
    return {"token": ((y + step + YS) % YS) * CORES + core}


def twin():
    _, _, y, core = place()
    return {"token": y * CORES + 1 - core}


def greet():
    barrier = pltpu.get_barrier_semaphore()
    others = [along_z(1), along_z(-1), mate(), holder(), along_y(1), along_y(-1), twin()]
    for other in others:
        pl.semaphore_signal(barrier, inc=1, device_id=other, device_id_type=MESH)
    pl.semaphore_wait(barrier, len(others))


class Wires:
    def __init__(self, send_sems, recv_sems):
        self.send_sems, self.recv_sems, self.slots, self.started = send_sems, recv_sems, {}, []

    def copy(self, key, src, dst, device):
        slot = self.slots.setdefault(key, len(self.slots))
        return pltpu.make_async_remote_copy(
            src_ref=src,
            dst_ref=dst,
            send_sem=self.send_sems.at[slot],
            recv_sem=self.recv_sems.at[slot],
            device_id=device,
            device_id_type=MESH,
        )

    def start(self, key, src, dst, device):
        made = self.copy(key, src, dst, device)
        made.start()
        self.started.append(made)

    def arrive(self, key, dst, device):
        self.copy(key, dst, dst, device).wait_recv()

    def drain(self):
        for made in self.started:
            made.wait_send()
        self.started = []


class Fetch:
    def __init__(self, wires, name, src, dst, lanes, first_lane=0):
        self.wires, self.name, self.src, self.dst, self.lanes, self.first_lane = wires, name, src, dst, lanes, first_lane
        self.size = src.shape[1 if lanes else 0] // (YS * CORES)

    def cut(self, ref, number, part, offset):
        size = self.size if part is None else self.size // 2
        start = pl.multiple_of(number * self.size, self.size) + (0 if part in (None, 0) else size)
        start = pl.multiple_of(start, size)
        if self.lanes:
            return ref.at[:, pl.ds(start, size)]
        return ref.at[pl.ds(start, size), pl.ds(offset, self.src.shape[1])]

    def slot(self, dy, dc, part=None):
        _, _, y, core = place()
        number = ((y + dy + YS) % YS) * CORES + (core if dc == 0 else 1 - core)
        return self.cut(self.dst, number, part, self.first_lane)

    def start(self, key, ref, device):
        self.wires.start((self.name, key), ref, ref, device)

    def arrive(self, key, ref):
        self.wires.arrive((self.name, key), ref, holder())

    def ask(self):
        _, _, y, core = place()
        self.wires.start((self.name, "x"), self.cut(self.src, y * CORES + core, None, 0), self.slot(0, 0), holder())

    def relay(self):
        self.arrive("x", self.slot(0, 0))
        self.start("y3", self.slot(0, 0), along_y(1))
        self.start("y1", self.slot(0, 0), along_y(-1))
        self.start("c0", self.slot(0, 0), twin())

    def pass_on(self):
        self.arrive("y3", self.slot(3, 0))
        self.start("h0", self.slot(3, 0, 0), along_y(1))
        self.start("c3", self.slot(3, 0), twin())
        self.arrive("y1", self.slot(1, 0))
        self.start("h1", self.slot(1, 0, 1), along_y(-1))
        self.start("c1", self.slot(1, 0), twin())

    def settle(self):
        self.arrive("h0", self.slot(2, 0, 0))
        self.arrive("h1", self.slot(2, 0, 1))
        self.start("c2", self.slot(2, 0), twin())

    def finish(self):
        for dy in (0, 3, 1, 2):
            self.arrive("c%d" % dy, self.slot(dy, 1))


def gather(wires, blocks, hook):
    rows = blocks.shape[3]
    low, high = pl.ds(0, rows // 2), pl.ds(rows // 2, rows // 2)
    up, down = 1, -1

    def full(h, dz, m):
        return blocks.at[h, dz, m]

    def spread(h, m):
        wires.start(("s", h, 3, m), full(h, 0, m), full(h, 3, m), along_z(up))
        wires.start(("s", h, 1, m), full(h, 0, m), full(h, 1, m), along_z(down))

    def to_mate(h, dz):
        wires.start(("m", h, dz), full(h, dz, 0), full(h, dz, 1), mate())

    def relay(h, m, onward):
        wires.arrive(("s", h, 3, m), full(h, 3, m), along_z(down))
        wires.start(("t", h, 0, m), blocks.at[h, 3, m, low], blocks.at[h, 2, m, low], along_z(up))
        if onward:
            to_mate(h, 3)
        wires.arrive(("s", h, 1, m), full(h, 1, m), along_z(up))
        wires.start(("t", h, 1, m), blocks.at[h, 1, m, high], blocks.at[h, 2, m, high], along_z(down))
        if onward:
            to_mate(h, 1)

    def last(h, m):
        wires.arrive(("t", h, 0, m), blocks.at[h, 2, m, low], along_z(down))
        wires.arrive(("t", h, 1, m), blocks.at[h, 2, m, high], along_z(up))

    to_mate(0, 0)
    spread(1, 0)
    spread(0, 0)
    to_mate(1, 0)
    hook("sent")
    wires.arrive(("m", 0, 0), full(0, 0, 1), mate())
    spread(0, 1)
    relay(1, 0, True)
    relay(0, 0, False)
    hook("early")
    wires.arrive(("m", 1, 0), full(1, 0, 1), mate())
    hook("own pair")
    last(1, 0)
    to_mate(1, 2)
    relay(0, 1, False)
    hook("middle")
    wires.arrive(("m", 1, 3), full(1, 3, 1), mate())
    wires.arrive(("m", 1, 1), full(1, 1, 1), mate())
    hook("sides")
    last(0, 0)
    last(0, 1)
    wires.arrive(("m", 1, 2), full(1, 2, 1), mate())
    hook("far")


def scatter(wires, out, bufs, produce, hook):
    z_half, z_full, mate0, mate1, e_half, e_full = bufs
    rows = out.shape[3]
    low, high = pl.ds(0, rows // 2), pl.ds(rows // 2, rows // 2)
    ways = ((0, 1, low, 1), (1, 3, high, -1))
    f32 = jnp.float32

    def wide(ref):
        return ref[...].astype(f32)

    def add_to(ref, *others):
        total = wide(ref)
        for other in others:
            total = total + wide(other)
        ref[...] = total.astype(ref.dtype)

    def mate_send(dz):
        wires.start(("m1", dz), out.at[1, dz, 1], mate1.at[dz], mate())

    def mate_join(dz):
        wires.arrive(("m1", dz), mate1.at[dz], mate())
        add_to(out.at[1, dz, 0], mate1.at[dz])

    produce(1, (2,))
    mate_send(2)
    produce(0, (2,))
    for m in (1, 0):
        for way, dz, part, step in ways:
            wires.start(("a", way, m), out.at[0, 2, m, part], z_half.at[way, m], along_z(step))
    produce(0, (1, 3))
    produce(1, (1, 3))
    mate_send(1)
    mate_send(3)
    mate_join(2)
    for way, dz, part, step in ways:
        wires.start(("e", way), out.at[1, 2, 0, part], e_half.at[way], along_z(step))
    for m in (1, 0):
        for way, dz, part, step in ways:
            wires.arrive(("a", way, m), z_half.at[way, m], along_z(-step))
            add_to(out.at[0, dz, m, part], z_half.at[way, m])
            wires.start(("b", way, m), out.at[0, dz, m], z_full.at[way, m], along_z(step))
    produce(1, (0,))
    mate_send(0)
    produce(0, (0,))
    hook("early")
    for way, dz, part, step in ways:
        mate_join(dz)
        wires.arrive(("e", way), e_half.at[way], along_z(-step))
        add_to(out.at[1, dz, 0, part], e_half.at[way])
        wires.start(("f", way), out.at[1, dz, 0], e_full.at[way], along_z(step))
    hook("middle")
    for way, dz, part, step in ways:
        wires.arrive(("b", way, 1), z_full.at[way, 1], along_z(-step))
    add_to(out.at[0, 0, 1], z_full.at[0, 1], z_full.at[1, 1])
    wires.start(("m0",), out.at[0, 0, 1], mate0, mate())
    hook("late")
    for way, dz, part, step in ways:
        wires.arrive(("b", way, 0), z_full.at[way, 0], along_z(-step))
    first = wide(out.at[0, 0, 0]) + wide(z_full.at[0, 0]) + wide(z_full.at[1, 0])
    wires.arrive(("m1", 0), mate1.at[0], mate())
    second = wide(out.at[1, 0, 0]) + wide(mate1.at[0])
    for way, dz, part, step in ways:
        wires.arrive(("f", way), e_full.at[way], along_z(-step))
        second = second + wide(e_full.at[way])
    wires.arrive(("m0",), mate0, mate())
    first = first + wide(mate0)
    return first, second


def norm_halves(rows, gain, width):
    mean_square = jnp.mean(rows * rows, axis=-1, keepdims=True)
    normed = (rows * lax.rsqrt(mean_square + EPSILON) * gain).astype(jnp.bfloat16)
    return normed[:, :width], normed[:, width:]


def stacked(blocks, h, dzs):
    rows, width = blocks.shape[3], blocks.shape[4]
    parts = [blocks[h, dz].reshape(2 * rows, width) for dz in dzs]
    return parts[0] if len(parts) == 1 else jnp.concatenate(parts, axis=0)


def project_kernel(
    tokens_ref, gain_ref, cos_ref, sin_ref, wq_hbm, wkv_hbm, wo_hbm, q_ref, kv_ref, wo_other,
    weights, others, blocks, load_sems, send_sems, recv_sems,
):
    rows, half_width = blocks.shape[3], blocks.shape[4]
    qcols = wq_hbm.shape[1]
    cols = qcols + wkv_hbm.shape[1]
    z, x, _, _ = place()
    loads = [
        pltpu.make_async_copy(wq_hbm, weights.at[:, pl.ds(0, qcols)], load_sems.at[0]),
        pltpu.make_async_copy(wkv_hbm, weights.at[:, pl.ds(qcols, cols - qcols)], load_sems.at[1]),
    ]
    for load in loads:
        load.start()
    first, second = norm_halves(tokens_ref[...].astype(jnp.float32), gain_ref[...], half_width)
    blocks[0, 0, 0] = first
    blocks[1, 0, 0] = second
    greet()
    wires = Wires(send_sems, recv_sems)
    fetch_q = Fetch(wires, "q", wq_hbm, others, False, 0)
    fetch_kv = Fetch(wires, "kv", wkv_hbm, others, False, qcols)
    fetch_o = Fetch(wires, "o", wo_hbm, wo_other, True)

    def emit(dzs, mine):
        shard = weights if mine else others
        part = sum(
            jnp.dot(
                stacked(blocks, h, dzs),
                shard[h * half_width : (h + 1) * half_width, :],
                preferred_element_type=jnp.float32,
            )
            for h in range(2)
        )
        is_key = (x % 2 == 0) if mine else (x % 2 == 1)
        which = x % 2 if mine else 1 - x % 2
        first_col = 0 if mine else qcols
        for i, dz in enumerate(dzs):
            for m in range(2):
                whole = part[(2 * i + m) * rows : (2 * i + m + 1) * rows]
                zz = (z + dz) % SIDE
                mm = x // 2 if m == 0 else 1 - x // 2
                cosine, sine = cos_ref[zz, mm], sin_ref[zz, mm]
                for head in range(qcols // HEAD_DIM):
                    piece = whole[:, head * HEAD_DIM : (head + 1) * HEAD_DIM]
                    turned = piece * cosine + pltpu.roll(piece, HEAD_DIM // 2, 1) * sine
                    at = first_col + head * HEAD_DIM
                    q_ref[zz, mm, :, at : at + HEAD_DIM] = turned.astype(jnp.bfloat16)
                piece = whole[:, qcols:]
                turned = piece * cosine + pltpu.roll(piece, HEAD_DIM // 2, 1) * sine
                kv_ref[which, zz, mm] = jnp.where(is_key, turned, piece).astype(jnp.bfloat16)

    def hook(name):
        if name == "sent":
            for fetch in (fetch_q, fetch_kv, fetch_o):
                fetch.ask()
        elif name == "early":
            fetch_q.relay()
            fetch_kv.relay()
            for load in loads:
                load.wait()
        elif name == "own pair":
            emit((0,), True)
        elif name == "middle":
            fetch_q.pass_on()
            fetch_kv.pass_on()
            fetch_o.relay()
        elif name == "sides":
            emit((3, 1), True)
            fetch_q.settle()
            fetch_kv.settle()
            fetch_q.finish()
            fetch_kv.finish()
            emit((0,), False)
            emit((3, 1), False)
            fetch_o.pass_on()
        else:
            emit((2,), True)
            emit((2,), False)
            fetch_o.settle()
            fetch_o.finish()

    gather(wires, blocks, hook)
    wires.drain()


def project(tokens, gain, cosine, sine, w_query, w_keyval, w_out):
    rows, width = tokens.shape
    cols = w_query.shape[1] + w_keyval.shape[1]
    vmem = pl.BlockSpec(memory_space=pltpu.VMEM)
    hbm = pl.BlockSpec(memory_space=pl.ANY)
    bf16 = jnp.bfloat16
    return pl.pallas_call(
        project_kernel,
        out_shape=(
            jax.ShapeDtypeStruct((SIDE, 2, rows, 2 * w_query.shape[1]), bf16),
            jax.ShapeDtypeStruct((2, SIDE, 2, rows, w_keyval.shape[1]), bf16),
            jax.ShapeDtypeStruct(w_out.shape, bf16),
        ),
        in_specs=[vmem] * 4 + [hbm] * 3,
        out_specs=(vmem, vmem, hbm),
        scratch_shapes=[
            pltpu.VMEM((width, cols), bf16),
            pltpu.VMEM((width, cols), bf16),
            pltpu.VMEM((2, SIDE, 2, rows, width // 2), bf16),
            pltpu.SemaphoreType.DMA((2,)),
            pltpu.SemaphoreType.DMA((64,)),
            pltpu.SemaphoreType.DMA((64,)),
        ],
        compiler_params=pltpu.CompilerParams(
            collective_id=0, has_side_effects=True, vmem_limit_bytes=48 << 20
        ),
        name="project",
    )(tokens, gain, cosine, sine, w_query, w_keyval, w_out)


def finish_kernel(
    tokens_ref, attn_ref, gain_ref, wo_hbm, wo2_hbm, wg_hbm, wu_hbm, wd_hbm, out_ref,
    wo, wg, wu, wd, wg2, wu2, wd2, blocks, hidden, hidden2, sending,
    z_half, z_full, mate0, mate1, e_half, e_full, state, load_sems, send_sems, recv_sems,
):
    rows, half_width = blocks.shape[3], blocks.shape[4]
    own = wo_hbm.shape[0]
    z, x, _, _ = place()
    loads = [
        pltpu.make_async_copy(src, dst, load_sems.at[i])
        for i, (src, dst) in enumerate(
            ((wo_hbm, wo.at[pl.ds(0, own)]), (wo2_hbm, wo.at[pl.ds(own, own)]), (wg_hbm, wg), (wu_hbm, wu), (wd_hbm, wd))
        )
    ]
    for load in loads:
        load.start()
    greet()
    bufs = (z_half, z_full, mate0, mate1, e_half, e_full)
    weight_wires = Wires(send_sems.at[3], recv_sems.at[3])
    fetch_g = Fetch(weight_wires, "g", wg_hbm, wg2, True)
    fetch_u = Fetch(weight_wires, "u", wu_hbm, wu2, True)
    fetch_d = Fetch(weight_wires, "d", wd_hbm, wd2, True)
    fetch_g.ask()
    fetch_u.ask()
    loads[0].wait()
    loads[1].wait()

    def columns(h):
        return pl.ds(h * half_width, half_width)

    def keep(h, dzs, part):
        for i, dz in enumerate(dzs):
            piece = part[2 * i * rows : 2 * (i + 1) * rows].astype(jnp.bfloat16)
            sending[h, dz] = piece.reshape(2, rows, half_width)

    def project_out(h, dzs):
        mine, other = x // 2, 1 - x // 2
        left = [attn_ref[(z + dz) % SIDE, m] for dz in dzs for m in (mine, other)]
        left = jnp.concatenate(left, axis=0)
        keep(h, dzs, jnp.dot(left, wo[:, columns(h)], preferred_element_type=jnp.float32))

    def hook_out(name):
        if name == "early":
            fetch_g.relay()
        elif name == "middle":
            fetch_g.pass_on()
        else:
            fetch_u.relay()

    out_wires = Wires(send_sems.at[0], recv_sems.at[0])
    first, second = scatter(out_wires, sending, bufs, project_out, hook_out)
    for h, proj in enumerate((first, second)):
        state[:, columns(h)] = (tokens_ref[:, columns(h)].astype(jnp.float32) + proj).astype(jnp.bfloat16)
    first, second = norm_halves(state[...].astype(jnp.float32), gain_ref[...], half_width)
    blocks[0, 0, 0] = first
    blocks[1, 0, 0] = second

    def gated(dzs, mine):
        gates, ups, result = (wg, wu, hidden) if mine else (wg2, wu2, hidden2)
        gate = upward = 0.0
        for h in range(2):
            left = stacked(blocks, h, dzs)
            across = (((1,), (1,)), ((), ()))
            gate = gate + lax.dot_general(left, gates[:, columns(h)], across, preferred_element_type=jnp.float32)
            upward = upward + lax.dot_general(left, ups[:, columns(h)], across, preferred_element_type=jnp.float32)
        value = (gate / (1.0 + jnp.exp(-gate)) * upward).astype(jnp.bfloat16)
        for i, dz in enumerate(dzs):
            result[dz] = value[2 * i * rows : 2 * (i + 1) * rows].reshape(2, rows, value.shape[1])

    def hook_gated(name):
        if name == "sent":
            fetch_d.ask()
            fetch_g.settle()
            loads[2].wait()
            loads[3].wait()
        elif name == "early":
            fetch_u.pass_on()
            fetch_g.finish()
        elif name == "own pair":
            gated((0,), True)
            fetch_d.relay()
        elif name == "middle":
            fetch_u.settle()
        elif name == "sides":
            gated((3, 1), True)
            fetch_u.finish()
            gated((0,), False)
            gated((3, 1), False)
            fetch_d.pass_on()
        else:
            gated((2,), True)
            gated((2,), False)
            fetch_d.settle()
            fetch_d.finish()
            loads[4].wait()

    gather_wires = Wires(send_sems.at[1], recv_sems.at[1])
    gather(gather_wires, blocks, hook_gated)
    out_wires.drain()

    def project_down(h, dzs):
        part = 0.0
        for values, weights in ((hidden, wd), (hidden2, wd2)):
            left = [values[dz].reshape(2 * rows, values.shape[3]) for dz in dzs]
            left = left[0] if len(left) == 1 else jnp.concatenate(left, axis=0)
            part = part + jnp.dot(left, weights[:, columns(h)], preferred_element_type=jnp.float32)
        keep(h, dzs, part)

    down_wires = Wires(send_sems.at[2], recv_sems.at[2])
    down = scatter(down_wires, sending, bufs, project_down, lambda name: None)
    for h in range(2):
        out_ref[:, columns(h)] = (state[:, columns(h)].astype(jnp.float32) + down[h]).astype(jnp.bfloat16)
    for wires in (gather_wires, down_wires, weight_wires):
        wires.drain()


def finish(tokens, attn, gain, w_out, w_out_other, w_gate, w_up, w_down):
    rows, width = tokens.shape
    hidden = w_gate.shape[0]
    vmem = pl.BlockSpec(memory_space=pltpu.VMEM)
    hbm = pl.BlockSpec(memory_space=pl.ANY)
    half = width // 2
    bf16 = jnp.bfloat16
    return pl.pallas_call(
        finish_kernel,
        out_shape=jax.ShapeDtypeStruct((rows, width), bf16),
        in_specs=[vmem] * 3 + [hbm] * 5,
        out_specs=vmem,
        scratch_shapes=[
            pltpu.VMEM((2 * w_out.shape[0], width), bf16),
            *[pltpu.VMEM((hidden, width), bf16)] * 6,
            pltpu.VMEM((2, SIDE, 2, rows, half), bf16),
            pltpu.VMEM((SIDE, 2, rows, hidden), bf16),
            pltpu.VMEM((SIDE, 2, rows, hidden), bf16),
            pltpu.VMEM((2, SIDE, 2, rows, half), bf16),
            pltpu.VMEM((2, 2, rows // 2, half), bf16),
            pltpu.VMEM((2, 2, rows, half), bf16),
            pltpu.VMEM((rows, half), bf16),
            pltpu.VMEM((SIDE, rows, half), bf16),
            pltpu.VMEM((2, rows // 2, half), bf16),
            pltpu.VMEM((2, rows, half), bf16),
            pltpu.VMEM((rows, width), bf16),
            pltpu.SemaphoreType.DMA((5,)),
            pltpu.SemaphoreType.DMA((4, 48)),
            pltpu.SemaphoreType.DMA((4, 48)),
        ],
        compiler_params=pltpu.CompilerParams(
            collective_id=1, has_side_effects=True, vmem_limit_bytes=60 << 20
        ),
        name="finish",
    )(tokens, attn, gain, w_out, w_out_other, w_gate, w_up, w_down)


def attend_kernel(bounds, q_ref, k_ref, v_ref, first_ref, last_ref, o_ref, *, qblk):
    block = pl.program_id(0)
    low, high, clear_low, clear_high = (bounds[i, block] for i in range(4))
    heads = q_ref.shape[1] // HEAD_DIM
    rows = heads * qblk
    factor = math.log2(math.e) / math.sqrt(HEAD_DIM)
    query = jnp.concatenate([q_ref[:, h * HEAD_DIM : (h + 1) * HEAD_DIM] for h in range(heads)], axis=0)
    first = jnp.concatenate([first_ref[...]] * heads, axis=0)
    last = jnp.concatenate([last_ref[...]] * heads, axis=0)

    def advance(masked, number, carry):
        peak, totals, summed = carry
        start = pl.multiple_of(number * KBLK, KBLK)
        keys = k_ref[pl.ds(start, KBLK), :]
        values = v_ref[pl.ds(start, KBLK), :]
        scores = lax.dot_general(query, keys, (((1,), (1,)), ((), ())), preferred_element_type=jnp.float32) * factor
        if masked:
            spots = lax.broadcasted_iota(jnp.int32, (rows, KBLK), 1) + start
            scores = jnp.where((spots >= first) & (spots <= last), scores, NEGATIVE)
        new_peak = jnp.maximum(peak, jnp.max(scores, axis=1, keepdims=True))
        decay = jnp.exp2(peak - new_peak)
        weights = jnp.exp2(scores - new_peak)
        totals = totals * decay + jnp.sum(weights, axis=1, keepdims=True)
        summed = summed * decay + jnp.dot(weights.astype(jnp.bfloat16), values, preferred_element_type=jnp.float32)
        return new_peak, totals, summed

    carry = (
        jnp.full((rows, 1), NEGATIVE, jnp.float32),
        jnp.zeros((rows, 1), jnp.float32),
        jnp.zeros((rows, HEAD_DIM), jnp.float32),
    )
    carry = lax.fori_loop(low, clear_low, functools.partial(advance, True), carry)
    carry = lax.fori_loop(clear_low, clear_high, functools.partial(advance, False), carry)
    peak, totals, summed = lax.fori_loop(clear_high, high, functools.partial(advance, True), carry)
    answer = (summed / totals).astype(jnp.bfloat16)
    for h in range(heads):
        o_ref[:, h * HEAD_DIM : (h + 1) * HEAD_DIM] = answer[h * qblk : (h + 1) * qblk]


def attend(queries, keys, values, first, last, bounds, qblk):
    total, cols = queries.shape
    whole = pl.BlockSpec(memory_space=pltpu.VMEM)
    return pl.pallas_call(
        functools.partial(attend_kernel, qblk=qblk),
        out_shape=jax.ShapeDtypeStruct((total, cols), jnp.bfloat16),
        grid_spec=pltpu.PrefetchScalarGridSpec(
            num_scalar_prefetch=1,
            grid=(total // qblk,),
            in_specs=[
                pl.BlockSpec((qblk, cols), lambda i, b: (i, 0)),
                whole,
                whole,
                pl.BlockSpec((qblk, 1), lambda i, b: (i, 0)),
                pl.BlockSpec((qblk, 1), lambda i, b: (i, 0)),
            ],
            out_specs=pl.BlockSpec((qblk, cols), lambda i, b: (i, 0)),
        ),
        compiler_params=pltpu.CompilerParams(vmem_limit_bytes=40 << 20),
        name="attend",
    )(bounds, queries, keys, values, first, last)


def body(tokens, doc_lengths, attn_gain, mlp_gain, w_query, w_keyval, w_out, w_gate, w_up, w_down):
    token_index = lax.axis_index("token")
    x = lax.axis_index("tensor") % SIDE
    rows = tokens.shape[0]
    qblk = 2 * rows
    block_rows = rows * SIDE * SIDE
    outer = (x == 0) | (x == SIDE - 1)
    lows, highs = jnp.where(outer, 0, 1), jnp.where(outer, SIDE - 1, SIDE - 2)
    runs = token_index * block_rows + jnp.arange(SIDE, dtype=jnp.int32) * (SIDE * rows)
    blocks = runs[:, None] + jnp.stack([lows, highs])[None, :] * rows
    spots = (blocks[:, :, None] + jnp.arange(rows, dtype=jnp.int32)).reshape(-1).astype(jnp.int32)
    ends = jnp.cumsum(doc_lengths)
    passed = spots[:, None] >= ends[None, :-1]
    first = jnp.max(jnp.where(passed, ends[None, :-1], 0), axis=1).astype(jnp.int32)
    position = (spots - first).astype(jnp.float32)
    half = HEAD_DIM // 2
    freq = jnp.exp(-math.log(ROPE_BASE) * jnp.arange(half, dtype=jnp.float32) * (2.0 / HEAD_DIM))
    angle = position[:, None] * freq[None, :]
    cosine, sine = jnp.cos(angle), jnp.sin(angle)
    cosine = jnp.concatenate([cosine, cosine], axis=1).reshape(SIDE, 2, rows, HEAD_DIM)
    sine = jnp.concatenate([-sine, sine], axis=1).reshape(SIDE, 2, rows, HEAD_DIM)
    queries, own, w_out_other = project(tokens, attn_gain[None, :], cosine, sine, w_query, w_keyval, w_out)
    queries = queries.reshape(SIDE * qblk, -1)
    count = SIDE * SIDE
    other = lax.ppermute(own, "tensor", [(i, i ^ 1) for i in range(count)])
    wide, narrow = jnp.where(outer, own, other), jnp.where(outer, other, own)
    both = jnp.stack([wide[:, :, 0], narrow[:, :, 0], narrow[:, :, 1], wide[:, :, 1]], axis=2)
    both = both.reshape(2, block_rows, HEAD_DIM)
    both = lax.all_gather(both, "token", axis=1, tiled=True)
    low = first[::qblk] // KBLK
    high = spots[qblk - 1 :: qblk] // KBLK + 1
    clear_low = jnp.minimum((first[qblk - 1 :: qblk] + KBLK - 1) // KBLK, high)
    clear_high = jnp.maximum(spots[::qblk] // KBLK, clear_low)
    bounds = jnp.stack([low, high, clear_low, clear_high]).astype(jnp.int32)
    attn = attend(queries, both[0], both[1], first[:, None], spots[:, None], bounds, qblk)
    attn = attn.reshape(SIDE, 2, rows, attn.shape[1])
    return finish(tokens, attn, mlp_gain[None, :], w_out, w_out_other, w_gate.T, w_up.T, w_down)


def solution(mesh):
    return jax.shard_map(
        body,
        mesh=mesh,
        in_specs=(
            P(("token", "tensor"), None),
            P(),
            P(),
            P(),
            P(None, "tensor"),
            P(None, "tensor"),
            P("tensor", None),
            P(None, "tensor"),
            P(None, "tensor"),
            P("tensor", None),
        ),
        out_specs=P(("token", "tensor"), None),
        check_vma=False,
    )
```

time: 276 us -> 242 us (0.88)
  the two profiles are of different devices: /device:TPU:9 before, /device:TPU:0 now
where the time goes in v2:
time: 242 us; the launch traced here: 239 us
  Pallas kernels  176 us (73%)
  waiting for transfers between devices  37.9 us (16%)
  between operations  13.5 us (6%)
  local copies, waits for them, and re-layouts  7.41 us (3%)
  other arithmetic  3.48 us (1%)
    pallas_call x1, Pallas kernels, finish(): pl.pallas_call(finish_kernel, out_shape=jax.ShapeDtypeStruct((rows, width...  123 us
    pallas_call x1, Pallas kernels, project(): pl.pallas_call(project_kernel, out_shape=(jax.ShapeDtypeStruct((SIDE, 2,...  47.3 us
    all_gather x1, waiting for transfers between devices, body(): both = lax.all_gather(both, 'token', axis=1, tiled=True)  29.6 us
    ppermute x1, waiting for transfers between devices, body(): other = lax.ppermute(own, 'tensor', [(i, i ^ 1) for i in range(count)])  8.3 us
    pallas_call x1, Pallas kernels, attend(): pl.pallas_call(functools.partial(attend_kernel, qblk=qblk), out_shape=jax...  6.29 us
  transfers between devices with their start and end apart: 2, of which 2 were waited for; matrix products, arithmetic and copies ran while one was open for 0% of the time, Pallas kernels for 0%

profile of v2, /device:TPU:0, one launch (start us, length us, event | category | flops | bytes accessed | tf_op | source)
XLA Modules:
  0.0 239.1 jit_solution(10963716700712005861)
XLA Ops:
  6.5 0.0 all-gather.2.cloned.1.call-start
  6.6 0.1 add_multiply_fusion
  6.7 0.1 broadcast_add_fusion
  6.7 0.1 iota_add_fusion
  6.8 0.1 add.82
  6.9 1.0 reduce-window.4
  7.9 0.1 select_reduce_fusion
  7.9 0.1 reduce_max.14
  8.0 0.1 subtract_convert_fusion
  8.1 1.0 fusion
  9.1 0.2 pad_maximum_fusion.1
  9.3 0.0 copy-done.4
  9.3 0.0 copy-done.1
  9.3 47.3 %project.1 = (bf16[4,2,64,512]{3,2,1,0:T(8,128)(2,1)S(1)}, bf16[2,4,2,64,128]{4,3,2,1,0:T(8,128)(2,1)S(1)}, bf16[256,4096]{1,0:T(8,128)(2,1)S(1)}) custom-call(bf16[64,4096]{1,0:T(8,128)(2,1)S(1)} %copy-done.1, f32[1,4096]{1,0:T(1,128)S(1)} %bitcast.25, f32[4,2,64,128]{3,2,1,0:T(8,128)S(1)} %get-tuple-element.23.cos_ref, ...), custom_call_target="tpu_custom_call" | custom-call | tf_op jit(solution)/shard_map/project/pallas_call | solution.py:368
  56.7 1.3 copy-done
  58.0 0.3 collective-permute-start
  58.3 8.3 %collective-permute-done = bf16[2,4,2,64,128]{4,3,2,1,0:T(8,128)(2,1)S(1)} collective-permute-done((bf16[2,4,2,64,128]{4,3,2,1,0:T(8,128)(2,1)S(1)}, bf16[2,4,2,64,128]{4,3,2,1,0:T(8,128)(2,1)S(1)}, u32[]{:S(2)}, u32[]{:S(2)}) %collective-permute-start) | collective-permute-done | bytes 262176 | tf_op jit(solution)/shard_map/ppermute | solution.py:631
  66.7 0.9 pad_maximum_fusion
  67.6 0.0 all-gather.2.cloned.1.call-update
  67.6 0.2 add.85.last_ref
  67.8 0.1 slice.35
  67.9 0.1 slice.34
  68.0 0.1 slice.36
  68.1 0.1 slice.33
  68.2 0.1 copy.13.first_ref
  68.4 29.6 %all-gather.2.cloned.1.call-done = bf16[2,8192,128]{2,1,0:T(8,128)(2,1)} async-done(((bf16[2,1024,128]{2,1,0:T(8,128)(2,1)}), bf16[2,8192,128]{2,1,0:T(8,128)(2,1)}) %all-gather.2.cloned.1.call-update) | async-done | bytes 4194320 | tf_op jit(solution)/shard_map/all_gather | solution.py:635
  98.0 2.5 %slice_bitcast_fusion = (bf16[8192,128]{1,0:T(8,128)(2,1)S(1)}, bf16[8192,128]{1,0:T(8,128)(2,1)S(1)}) fusion(bf16[2,8192,128]{2,1,0:T(8,128)(2,1)} %all-gather.2.cloned.1.call-done), kind=kLoop, calls=%fused_computation | loop fusion | bytes 8388608 | tf_op jit(solution)/shard_map/squeeze | solution.py:641
  100.5 6.3 %attend.1 = bf16[512,512]{1,0:T(8,128)(2,1)S(1)} custom-call(s32[4,4]{1,0:T(4,128)S(1)} %pad_add_fusion.bounds, bf16[512,512]{1,0:T(8,128)(2,1)S(1)} %bitcast.24, bf16[8192,128]{1,0:T(8,128)(2,1)S(1)} %get-tuple-element.15.k_ref, bf16[8192,128]{1,0:T(8,128)(2,1)S(1)} %get-tuple-element.14.v_ref, s32[512,1]{1,0:T(8,128)S(1)} %copy.13.first_ref, ...), custom_call_target="tpu_custom_call" | custom-call | tf_op jit(solution)/shard_map/attend/pallas_call | solution.py:587
  106.8 0.0 copy-start.2
  106.8 0.8 copy-done.2
  107.6 122.8 %finish.1 = bf16[64,4096]{1,0:T(8,128)(2,1)} custom-call(bf16[64,4096]{1,0:T(8,128)(2,1)} %tokens_ref.3, bf16[4,2,64,512]{3,2,1,0:T(8,128)(2,1)} %bitcast.23, f32[1,4096]{1,0:T(1,128)} %bitcast.30, bf16[256,4096]{1,0:T(8,128)(2,1)} %wo_hbm.3, bf16[256,4096]{1,0:T(8,128)(2,1)} %copy-done, bf16[448,4096]{1,0:T(8,128)(2,1)} %bitcast.26, ...), custom_call_target="tpu_custom_call" | custom-call | tf_op jit(solution)/shard_map/finish/pallas_call | solution.py:515
  230.4 1.9 copy.16
  (13 shorter events, 0.1 us)
Async XLA Ops:
  6.5 2.8 %copy-start.4 = (f32[4096]{0:T(1024)S(1)}, f32[4096]{0:T(1024)}, u32[]{:S(2)}) copy-start(f32[4096]{0:T(1024)} %param.12) | copy-start | bytes 49156
  6.5 2.8 %copy-start.1 = (bf16[64,4096]{1,0:T(8,128)(2,1)S(1)}, bf16[64,4096]{1,0:T(8,128)(2,1)}, u32[]{:S(2)}) copy-start(bf16[64,4096]{1,0:T(8,128)(2,1)} %tokens_ref.3) | copy-start | bytes 1572868
  6.5 2.8 %copy-start.3 = (bf16[4096,128]{1,0:T(8,128)(2,1)S(1)}, bf16[4096,128]{1,0:T(8,128)(2,1)}, u32[]{:S(2)}) copy-start(bf16[4096,128]{1,0:T(8,128)(2,1)} %wkv_hbm.1) | copy-start | bytes 3145732
  6.5 91.5 %all-gather.2.cloned.1.call-start = ((), (), s32[]{:S(2)}) async-start(), calls=%async_computation | async-start | bytes 4718592 | tf_op jit(solution)/shard_map/all_gather | solution.py:635
  56.7 1.3 copy-start
  58.0 8.7 %collective-permute-start = (bf16[2,4,2,64,128]{4,3,2,1,0:T(8,128)(2,1)S(1)}, bf16[2,4,2,64,128]{4,3,2,1,0:T(8,128)(2,1)S(1)}, u32[]{:S(2)}, u32[]{:S(2)}) collective-permute-start(bf16[2,4,2,64,128]{4,3,2,1,0:T(8,128)(2,1)S(1)} %get-tuple-element.9), channel_id=1, source_target_pairs={{0,1},{1,0},{2,3},{3,2},{4,5},{5,4},{6,7},{7,6},{8,9},{9,8},{10,11... | collective-permute-start | bytes 786440 | tf_op jit(solution)/shard_map/ppermute | solution.py:631
  106.8 0.8 copy-start.2
Sparse Core Ops, SparseCore 0:
  67.7 30.2 all-gather.1
